TPU v7x, 512 devices: a whole 4x4x16 slice. The times are simulated.
512 devices in a mesh: expert: 4 (over z_hi, core), rep: 4 (over y), hid: 32 (over x, z_lo).
Axes of the slice: x: 4, y: 4, z: 16 (z_hi: 2, z_lo: 8; z = z_hi * 8 + z_lo), core: 2. Of those that a mesh axis runs over, the one named last changes fastest.
Arguments:
- tokens: bfloat16 [1024, 6144], P(('expert', 'hid'), 'rep'), may hold values from -6 to 6
- norm_gain: float32 [6144], P('rep'), may hold values from 0.25 to 1.75
- expert_ids: int32 [1024, 2], P(('expert', 'hid')), may hold values from 0 to 3, as said below
- slot_ids: int32 [1024, 2], P(('expert', 'hid')), may hold values from 0 to 4, as said below
- w_gate: bfloat16 [4, 6144, 8192], P('expert', 'rep', 'hid'), may hold values from -0.078125 to 0.078125
- w_up: bfloat16 [4, 6144, 8192], P('expert', 'rep', 'hid'), may hold values from -0.078125 to 0.078125
- grad_gate: bfloat16 [4, 640, 8192], P('expert', None, 'hid'), may hold values from -1.1953125 to 1.1953125
- grad_up: bfloat16 [4, 640, 8192], P('expert', None, 'hid'), may hold values from -1.1953125 to 1.1953125
Outputs:
- grad_w_gate: bfloat16 [4, 6144, 8192], P('expert', 'rep', 'hid')
- grad_w_up: bfloat16 [4, 6144, 8192], P('expert', 'rep', 'hid')
- grad_tokens: bfloat16 [1024, 6144], P(('expert', 'hid'), 'rep')
Inputs may be any that keep to these rules, and one draw needn't show every extreme that they name: `expert_ids`: each token names two different experts; among the 8 tokens of one block, no expert is named more than 5 times and some expert exactly 5 times. Within one block of 8 tokens, the pairs (expert_ids[t, k], slot_ids[t, k]) are all different.
All inputs are finite; a program needn't handle non-finite values.
Results may differ from a plain program's by a relative error of at most 0.0049.
Values may be sent and summed in bfloat16 or wider, within the bound.
No kernel may reach another device: no remote copies, remote signals or barrier semaphores. Data moves between devices by JAX's collectives and lax.ppermute only.
A program may use at most 64 MiB of HBM per device.

v0:
```python
import jax
import jax.numpy as jnp
from jax import lax
from jax.sharding import PartitionSpec as P

D = 6144


def copy_for_each(x, axis):
    size = lax.axis_size(axis)
    return lax.all_to_all(jnp.broadcast_to(x[None], (size, *x.shape)), axis, 0, 0, tiled=True)


def of_everyone(x, axis):
    return copy_for_each(x, axis).sum(axis=0)


def feature_total(partial_value):
    return of_everyone(partial_value, "rep")


def on_device(tokens, norm_gain, expert_ids, slot_ids, w_gate, w_up, grad_gate, grad_up):
    groups = lax.axis_size("expert")
    block_tokens = tokens.shape[0]
    slot_count = 5 * block_tokens // (2 * groups)
    values = tokens.astype(jnp.float32)
    square_sums = feature_total(jnp.sum(values * values, axis=1))
    inverse_rms = lax.rsqrt(square_sums / D + 1e-05)[:, None]
    scaled_in = values * inverse_rms
    normed = (scaled_in * norm_gain).astype(jnp.bfloat16)
    slot_code = expert_ids * slot_count + slot_ids
    codes_all = jnp.arange(groups * slot_count, dtype=jnp.int32)
    onehot = (
        (slot_code[:, 0][None, :] == codes_all[:, None])
        | (slot_code[:, 1][None, :] == codes_all[:, None])
    ).astype(jnp.bfloat16)
    feat_width = normed.shape[1]
    outgoing = (
        jnp.dot(onehot, normed, preferred_element_type=jnp.float32)
        .astype(jnp.bfloat16)
        .reshape(groups, slot_count, feat_width)
    )
    arrived = lax.all_to_all(outgoing, "expert", split_axis=0, concat_axis=0, tiled=True)
    own_rows = arrived.reshape(groups * slot_count, feat_width)
    gate_cot = grad_gate[0]
    up_cot = grad_up[0]
    row_contract = (((0,), (0,)), ((), ()))
    gathered = lax.all_gather(own_rows, "hid", axis=0, tiled=True)
    gate_part = gate_cot
    up_part = up_cot
    new_gate = lax.dot_general(
        gathered, gate_part, row_contract, preferred_element_type=jnp.float32
    )
    new_up = lax.dot_general(gathered, up_part, row_contract, preferred_element_type=jnp.float32)
    unit_contract = (((1,), (1,)), ((), ()))
    gate_part = gate_cot
    up_part = up_cot
    first_term = lax.dot_general(
        gate_part, w_gate[0], unit_contract, preferred_element_type=jnp.float32
    )
    summed = lax.psum_scatter(
        first_term
        + lax.dot_general(up_part, w_up[0], unit_contract, preferred_element_type=jnp.float32),
        "hid",
        scatter_dimension=0,
        tiled=True,
    )
    returned_rows = lax.all_to_all(
        summed.astype(jnp.bfloat16).reshape(groups, slot_count, feat_width),
        "expert",
        split_axis=0,
        concat_axis=0,
        tiled=True,
    )
    normed_grad = jnp.dot(
        onehot.T,
        returned_rows.reshape(groups * slot_count, feat_width),
        preferred_element_type=jnp.float32,
    )
    scaled = normed_grad * norm_gain
    dotted = feature_total(jnp.sum(scaled * scaled_in, axis=1)) / D
    grad_tokens = (inverse_rms * (scaled - scaled_in * dotted[:, None])).astype(jnp.bfloat16)
    return (new_gate.astype(jnp.bfloat16)[None], new_up.astype(jnp.bfloat16)[None], grad_tokens)


def solution(mesh):
    placed = (
        P(("expert", "hid"), "rep"),
        P("rep"),
        P(("expert", "hid"), None),
        P(("expert", "hid"), None),
        P("expert", "rep", "hid"),
        P("expert", "rep", "hid"),
        P("expert", None, "hid"),
        P("expert", None, "hid"),
    )
    return jax.shard_map(
        on_device,
        mesh=mesh,
        in_specs=placed,
        out_specs=(
            P("expert", "rep", "hid"),
            P("expert", "rep", "hid"),
            P(("expert", "hid"), "rep"),
        ),
        check_vma=False,
    )
```

profile of v0, /device:TPU:8, one launch (start us, length us, event | category | flops | bytes accessed | tf_op | source)
XLA Modules:
  0.0 289.3 jit_solution(9607621341677522654)
XLA Ops:
  7.2 0.0 copy-start
  7.2 0.9 fusion.18
  8.1 0.6 broadcast_in_dim.8
  8.7 9.0 %all-to-all-start = ((f32[4,1,8]{2,1,0:T(1,128)}), f32[4,1,8]{2,1,0:T(1,128)S(1)}, u32[]{:S(2)}, u32[]{:S(2)}) async-start(f32[4,1,8]{2,1,0:T(1,128)} %broadcast_in_dim.8), calls=%async_computation | async-start | bytes 4096 | tf_op jit(solution)/shard_map/all_to_all | solution.py:11
  17.7 0.0 copy-done
  17.7 0.0 copy-start.6
  17.7 0.0 copy-start.7
  17.7 0.0 copy-start.2
  17.7 0.0 copy-start.5
  17.7 0.0 copy-start.1
  17.7 0.0 copy-start.4
  17.7 3.6 %fusion.4 = f32[640,1536]{1,0:T(8,128)} fusion(bf16[1,1536,256]{2,1,0:T(8,128)(2,1)S(1)} %copy-done, bf16[1,640,256]{2,1,0:T(8,128)(2,1)} %param.14), kind=kOutput, calls=%fused_computation.8 | convolution fusion | flops 503316480 | bytes 5046272 | tf_op jit(solution)/shard_map/dot_general | solution.py:58
  21.4 0.0 copy-done.6
  21.4 0.0 copy-done.7
  21.4 0.0 all-to-all-done
  21.5 0.0 copy-done.2
  21.5 0.0 copy-done.5
  21.5 0.2 convolution_convert_fusion.2
  21.7 0.7 reshape.41
  22.4 11.0 %all-to-all-start.1 = ((bf16[4,5,1536]{2,1,0:T(8,128)(2,1)}), bf16[4,5,1536]{2,1,0:T(8,128)(2,1)S(1)}, u32[]{:S(2)}, u32[]{:S(2)}) async-start(bf16[4,5,1536]{2,1,0:T(8,128)(2,1)} %reshape.41), calls=%async_computation.1 | async-start | bytes 196608 | tf_op jit(solution)/shard_map/all_to_all | solution.py:43
  33.4 0.0 all-gather.3.cloned.1.call-start
  33.4 0.0 copy-done.1
  33.4 0.0 copy-done.4
  33.4 4.7 %convolution_add_fusion = f32[640,1536]{1,0:T(8,128)} fusion(f32[640,1536]{1,0:T(8,128)} %fusion.4, bf16[1,1536,256]{2,1,0:T(8,128)(2,1)S(1)} %copy-done.1, bf16[1,640,256]{2,1,0:T(8,128)(2,1)S(1)} %copy-done.4), kind=kOutput, calls=%fused_computation | convolution fusion | flops 504299520 | bytes 8978432 | tf_op jit(solution)/shard_map/dot_general | solution.py:63
  38.1 8.4 %all-to-all-done.1 = bf16[4,5,1536]{2,1,0:T(8,128)(2,1)S(1)} async-done(((bf16[4,5,1536]{2,1,0:T(8,128)(2,1)}), bf16[4,5,1536]{2,1,0:T(8,128)(2,1)S(1)}, u32[]{:S(2)}, u32[]{:S(2)}) %all-to-all-start.1) | async-done | bytes 61472 | tf_op jit(solution)/shard_map/all_to_all | solution.py:43
  46.5 0.7 reshape.45
  47.1 0.0 all-gather.3.cloned.1.call-update
  47.1 160.0 %fusion = f32[24,1536]{1,0:T(8,128)S(1)} fusion(f32[640,1536]{1,0:T(8,128)} %convolution_add_fusion), kind=kCustom, calls=%all-reduce-scatter | all-reduce-scatter fusion | flops 1179649 | bytes 4081664
  207.1 1.3 collective-permute-start.5
  208.5 1.3 collective-permute-start
  209.8 1.3 collective-permute-start.1
  211.1 1.3 collective-permute-start.2
  212.4 8.9 %collective-permute-start.3 = (bf16[24,1536]{1,0:T(8,128)(2,1)S(1)}, bf16[24,1536]{1,0:T(8,128)(2,1)S(1)}, u32[]{:S(2)}, u32[]{:S(2)}) collective-permute-start(bf16[24,1536]{1,0:T(8,128)(2,1)S(1)} %convert.10), channel_id=1, source_target_pairs={{0,4},{1,5},{2,6},{3,7},{4,8},{5,9},{6,10},{7,11},{8,12},{9,13},{1... | collective-permute-start | bytes 221192
  221.2 0.0 collective-permute-done.5
  221.3 1.3 collective-permute-start.4
  222.6 1.3 dynamic-slice.4
  224.5 0.0 collective-permute-done
  224.5 0.0 collective-permute-done.1
  224.5 0.0 collective-permute-done.2
  224.5 0.0 collective-permute-done.3
  224.5 0.0 collective-permute-done.4
  224.5 1.1 concatenate
  225.7 21.8 %all_to_all.22 = bf16[4,5,1536]{2,1,0:T(8,128)(2,1)S(1)} all-to-all(bf16[4,5,1536]{2,1,0:T(8,128)(2,1)S(1)} %reshape.43), channel_id=1, replica_groups=mesh['expert'=4,'rep'=4,'hid'=32] {'expert'}, dimensions={0} | all-to-all | bytes 122880 | tf_op jit(solution)/shard_map/all_to_all | solution.py:68
  247.5 0.0 copy-start.3
  247.6 0.3 fusion.14
  247.9 8.3 %all_to_all.23 = f32[4,1,8]{2,1,0:T(1,128)S(1)} all-to-all(f32[4,1,8]{2,1,0:T(1,128)S(1)} %broadcast_in_dim.11), channel_id=1, replica_groups=mesh['expert'=4,'rep'=4,'hid'=32] {'rep'}, dimensions={0} | all-to-all | bytes 256 | tf_op jit(solution)/shard_map/all_to_all | solution.py:11
  256.2 0.7 fusion.17
  256.9 19.5 %all-gather.3.cloned.1.call-done = bf16[32,20,1536]{2,1,0:T(8,128)(2,1)} async-done(((bf16[1,20,1536]{2,1,0:T(8,128)(2,1)}), bf16[32,20,1536]{2,1,0:T(8,128)(2,1)}) %all-gather.3.cloned.1.call-update) | async-done | bytes 1966096 | tf_op jit(solution)/shard_map/all_gather | solution.py:48
  276.4 2.6 reshape.46
  279.0 0.0 copy-done.3
  279.0 1.7 fusion.1
  280.7 1.7 fusion.2
  (12 shorter events, 0.2 us)
Async XLA Ops:
  7.2 10.5 %copy-start = (bf16[1,1536,256]{2,1,0:T(8,128)(2,1)S(1)}, bf16[1,1536,256]{2,1,0:T(8,128)(2,1)}, u32[]{:S(2)}) copy-start(bf16[1,1536,256]{2,1,0:T(8,128)(2,1)} %param.12) | copy-start | bytes 2359300
  8.7 12.7 %all-to-all-start = ((f32[4,1,8]{2,1,0:T(1,128)}), f32[4,1,8]{2,1,0:T(1,128)S(1)}, u32[]{:S(2)}, u32[]{:S(2)}) async-start(f32[4,1,8]{2,1,0:T(1,128)} %broadcast_in_dim.8), calls=%async_computation | async-start | bytes 4096 | tf_op jit(solution)/shard_map/all_to_all | solution.py:11
  17.7 3.7 %copy-start.6 = (s32[8,2]{0,1:T(2,128)S(1)}, s32[8,2]{0,1:T(2,128)}, u32[]{:S(2)}) copy-start(s32[8,2]{0,1:T(2,128)} %param.11) | copy-start | bytes 196
  17.7 3.7 %copy-start.7 = (s32[8,2]{0,1:T(2,128)S(1)}, s32[8,2]{0,1:T(2,128)}, u32[]{:S(2)}) copy-start(s32[8,2]{0,1:T(2,128)} %param.10) | copy-start | bytes 196
  17.7 3.8 %copy-start.2 = (bf16[8,1536]{1,0:T(8,128)(2,1)S(1)}, bf16[8,1536]{1,0:T(8,128)(2,1)}, u32[]{:S(2)}) copy-start(bf16[8,1536]{1,0:T(8,128)(2,1)} %param.8) | copy-start | bytes 73732
  17.7 3.8 %copy-start.5 = (f32[1536]{0:T(1024)S(1)}, f32[1536]{0:T(1024)}, u32[]{:S(2)}) copy-start(f32[1536]{0:T(1024)} %param.9) | copy-start | bytes 18436
  17.7 15.7 %copy-start.1 = (bf16[1,1536,256]{2,1,0:T(8,128)(2,1)S(1)}, bf16[1,1536,256]{2,1,0:T(8,128)(2,1)}, u32[]{:S(2)}) copy-start(bf16[1,1536,256]{2,1,0:T(8,128)(2,1)} %param.13) | copy-start | bytes 2359300
  17.7 15.7 %copy-start.4 = (bf16[1,640,256]{2,1,0:T(8,128)(2,1)S(1)}, bf16[1,640,256]{2,1,0:T(8,128)(2,1)}, u32[]{:S(2)}) copy-start(bf16[1,640,256]{2,1,0:T(8,128)(2,1)} %param.15) | copy-start | bytes 983044
  22.4 24.1 %all-to-all-start.1 = ((bf16[4,5,1536]{2,1,0:T(8,128)(2,1)}), bf16[4,5,1536]{2,1,0:T(8,128)(2,1)S(1)}, u32[]{:S(2)}, u32[]{:S(2)}) async-start(bf16[4,5,1536]{2,1,0:T(8,128)(2,1)} %reshape.41), calls=%async_computation.1 | async-start | bytes 196608 | tf_op jit(solution)/shard_map/all_to_all | solution.py:43
  33.4 243.1 %all-gather.3.cloned.1.call-start = ((), (), s32[]{:S(2)}) async-start(), calls=%async_computation.4 | async-start | bytes 2433024 | tf_op jit(solution)/shard_map/all_gather | solution.py:48
  207.1 14.1 %collective-permute-start.5 = (bf16[4,1536]{1,0:T(4,128)(2,1)S(1)}, bf16[4,1536]{1,0:T(4,128)(2,1)S(1)}, u32[]{:S(2)}, u32[]{:S(2)}) collective-permute-start(bf16[4,1536]{1,0:T(4,128)(2,1)S(1)} %slice.8), channel_id=1, source_target_pairs={{0,6},{1,7},{2,8},{3,9},{4,10},{5,11},{6,12},{7,13},{8,14},{9,15},... | collective-permute-start | bytes 36872
  208.5 16.0 %collective-permute-start = (bf16[24,1536]{1,0:T(8,128)(2,1)S(1)}, bf16[24,1536]{1,0:T(8,128)(2,1)S(1)}, u32[]{:S(2)}, u32[]{:S(2)}) collective-permute-start(bf16[24,1536]{1,0:T(8,128)(2,1)S(1)} %convert.10), channel_id=1, source_target_pairs={{0,1},{1,2},{2,3},{3,4},{4,5},{5,6},{6,7},{7,8},{8,9},{9,10},{10,1... | collective-permute-start | bytes 221192
  209.8 14.7 %collective-permute-start.1 = (bf16[24,1536]{1,0:T(8,128)(2,1)S(1)}, bf16[24,1536]{1,0:T(8,128)(2,1)S(1)}, u32[]{:S(2)}, u32[]{:S(2)}) collective-permute-start(bf16[24,1536]{1,0:T(8,128)(2,1)S(1)} %convert.10), channel_id=1, source_target_pairs={{0,2},{1,3},{2,4},{3,5},{4,6},{5,7},{6,8},{7,9},{8,10},{9,11},{10,... | collective-permute-start | bytes 221192
  211.1 13.4 %collective-permute-start.2 = (bf16[24,1536]{1,0:T(8,128)(2,1)S(1)}, bf16[24,1536]{1,0:T(8,128)(2,1)S(1)}, u32[]{:S(2)}, u32[]{:S(2)}) collective-permute-start(bf16[24,1536]{1,0:T(8,128)(2,1)S(1)} %convert.10), channel_id=1, source_target_pairs={{0,3},{1,4},{2,5},{3,6},{4,7},{5,8},{6,9},{7,10},{8,11},{9,12},{10... | collective-permute-start | bytes 221192
  212.4 12.1 %collective-permute-start.3 = (bf16[24,1536]{1,0:T(8,128)(2,1)S(1)}, bf16[24,1536]{1,0:T(8,128)(2,1)S(1)}, u32[]{:S(2)}, u32[]{:S(2)}) collective-permute-start(bf16[24,1536]{1,0:T(8,128)(2,1)S(1)} %convert.10), channel_id=1, source_target_pairs={{0,4},{1,5},{2,6},{3,7},{4,8},{5,9},{6,10},{7,11},{8,12},{9,13},{1... | collective-permute-start | bytes 221192
  221.3 3.3 %collective-permute-start.4 = (bf16[24,1536]{1,0:T(8,128)(2,1)S(1)}, bf16[24,1536]{1,0:T(8,128)(2,1)S(1)}, u32[]{:S(2)}, u32[]{:S(2)}) collective-permute-start(bf16[24,1536]{1,0:T(8,128)(2,1)S(1)} %convert.10), channel_id=1, source_target_pairs={{0,5},{1,6},{2,7},{3,8},{4,9},{5,10},{6,11},{7,12},{8,13},{9,14},{... | collective-permute-start | bytes 221192
  247.5 31.5 %copy-start.3 = (bf16[1,640,256]{2,1,0:T(8,128)(2,1)S(1)}, bf16[1,640,256]{2,1,0:T(8,128)(2,1)}, u32[]{:S(2)}) copy-start(bf16[1,640,256]{2,1,0:T(8,128)(2,1)} %param.14) | copy-start | bytes 983044
Sparse Core Ops, SparseCore 0:
  47.3 229.1 all-gather.2
where the time goes:
time: 290 us; the launch traced here: 289 us
  blocking collectives  190 us (66%)
  starting transfers between devices  35.3 us (12%)
  waiting for transfers between devices  28 us (10%)
  between operations  14.9 us (5%)
  matrix products  12.3 us (4%)
  local copies, waits for them, and re-layouts  7.02 us (2%)
    unnamed x1, blocking collectives  160 us
    all_to_all x1, blocking collectives, on_device(): lax.all_to_all(summed.astype(jnp.bfloat16).reshape(groups, slot_count, fe...  21.8 us
    all_gather x1, waiting for transfers between devices, on_device(): gathered = lax.all_gather(own_rows, 'hid', axis=0, tiled=True)  19.5 us
    unnamed x6, starting transfers between devices  15.3 us
    all_to_all x1, starting transfers between devices, on_device(): lax.all_to_all(outgoing, 'expert', split_axis=0, concat_axis=0, tiled=True)  11 us
    all_to_all x1, starting transfers between devices, copy_for_each(): lax.all_to_all(jnp.broadcast_to(x[None], (size, *x.shape)), axis, 0, 0, t...  8.98 us
    all_to_all x1, waiting for transfers between devices, on_device(): lax.all_to_all(outgoing, 'expert', split_axis=0, concat_axis=0, tiled=True)  8.38 us
    all_to_all x1, blocking collectives, copy_for_each(): lax.all_to_all(jnp.broadcast_to(x[None], (size, *x.shape)), axis, 0, 0, t...  8.3 us
  transfers between devices with their start and end apart: 9, of which 2 were waited for; matrix products, arithmetic and copies ran while one was open for 59% of the time, Pallas kernels for 0%

commit v1 on v0

--- a/solution.py
+++ b/solution.py
@@ -45,7 +45,9 @@
     gate_cot = grad_gate[0]
     up_cot = grad_up[0]
     row_contract = (((0,), (0,)), ((), ()))
-    gathered = lax.all_gather(own_rows, "hid", axis=0, tiled=True)
+    gathered = jnp.concatenate(
+        lax.all_to_all(jnp.stack([own_rows] * lax.axis_size("hid")), "hid", 0, 0), axis=0
+    )
     gate_part = gate_cot
     up_part = up_cot
     new_gate = lax.dot_general(

time: 290 us -> 370 us (1.28)
  the two profiles are of different devices: /device:TPU:8 before, /device:TPU:32 now
where the time goes in v1:
time: 370 us
  blocking collectives  149 us (40%)
  waiting for transfers between devices  140 us (38%)
  starting transfers between devices  57.2 us (15%)
  matrix products  9.88 us (3%)
  local copies, waits for them, and re-layouts  9.69 us (3%)
    unnamed x1, blocking collectives  149 us
    all_to_all x1, waiting for transfers between devices, on_device(): lax.all_to_all(jnp.stack([own_rows] * lax.axis_size('hid')), 'hid', 0, 0)  105 us
    unnamed x6, starting transfers between devices  21.7 us
    all_to_all x1, starting transfers between devices, on_device(): lax.all_to_all(jnp.stack([own_rows] * lax.axis_size('hid')), 'hid', 0, 0)  13.9 us
    all_to_all x1, waiting for transfers between devices, on_device(): lax.all_to_all(outgoing, 'expert', split_axis=0, concat_axis=0, tiled=True)  12.6 us
    all_to_all x1, waiting for transfers between devices, on_device(): lax.all_to_all(summed.astype(jnp.bfloat16).reshape(groups, slot_count, fe...  12.1 us
    all_to_all x1, starting transfers between devices, on_device(): lax.all_to_all(summed.astype(jnp.bfloat16).reshape(groups, slot_count, fe...  9.61 us
    all_to_all x2, starting transfers between devices, copy_for_each(): lax.all_to_all(jnp.broadcast_to(x[None], (size, *x.shape)), axis, 0, 0, t...  8.64 us
  transfers between devices with their start and end apart: 11, of which 6 were waited for; matrix products, arithmetic and copies ran while one was open for 1% of the time, Pallas kernels for 0%

profile of v1, /device:TPU:32, one launch (start us, length us, event | category | flops | bytes accessed | tf_op | source)
XLA Modules:
  0.0 369.6 jit_solution(4485539712165382160)
XLA Ops:
  0.6 0.0 copy-start
  0.6 0.0 copy-start.2
  0.7 0.0 copy-start.5
  0.7 1.1 copy-done
  1.8 1.7 fusion.4
  3.5 0.0 copy-done.2
  3.5 0.0 copy-done.5
  3.5 2.6 convolution_add_fusion
  6.0 0.0 copy-start.3
  6.0 0.0 copy-start.8
  6.0 0.0 copy-start.9
  6.0 0.0 copy-start.7
  6.1 148.8 %fusion = f32[24,1536]{1,0:T(8,128)S(1)} fusion(f32[640,1536]{1,0:T(8,128)} %convolution_add_fusion), kind=kCustom, calls=%all-reduce-scatter | all-reduce-scatter fusion | flops 1179649 | bytes 4081664
  154.9 1.9 collective-permute-start
  156.8 1.3 collective-permute-start.1
  158.1 1.3 collective-permute-start.2
  159.4 7.5 %collective-permute-start.3 = (bf16[24,1536]{1,0:T(8,128)(2,1)S(1)}, bf16[24,1536]{1,0:T(8,128)(2,1)S(1)}, u32[]{:S(2)}, u32[]{:S(2)}) collective-permute-start(bf16[24,1536]{1,0:T(8,128)(2,1)S(1)} %convert.10), channel_id=1, source_target_pairs={{0,4},{1,5},{2,6},{3,7},{4,8},{5,9},{6,10},{7,11},{8,12},{9,13},{1... | collective-permute-start | bytes 221192
  166.9 6.4 %collective-permute-start.5 = (bf16[4,1536]{1,0:T(4,128)(2,1)S(1)}, bf16[4,1536]{1,0:T(4,128)(2,1)S(1)}, u32[]{:S(2)}, u32[]{:S(2)}) collective-permute-start(bf16[4,1536]{1,0:T(4,128)(2,1)S(1)} %slice.8), channel_id=1, source_target_pairs={{0,6},{1,7},{2,8},{3,9},{4,10},{5,11},{6,12},{7,13},{8,14},{9,15},... | collective-permute-start | bytes 36872
  173.3 0.0 copy-done.3
  173.3 0.1 fusion.18
  173.5 0.6 broadcast_in_dim.8
  174.0 5.4 %all-to-all-start = ((f32[4,1,8]{2,1,0:T(1,128)}), f32[4,1,8]{2,1,0:T(1,128)S(1)}, u32[]{:S(2)}, u32[]{:S(2)}) async-start(f32[4,1,8]{2,1,0:T(1,128)} %broadcast_in_dim.8), calls=%async_computation | async-start | bytes 4096 | tf_op jit(solution)/shard_map/all_to_all | solution.py:11
  179.5 0.0 copy-done.8
  179.5 0.0 copy-done.9
  179.5 1.3 dynamic-slice.4
  181.4 3.3 all-to-all-done
  184.7 0.0 collective-permute-done.5
  184.7 3.4 collective-permute-start.4
  188.1 0.0 collective-permute-done
  188.1 0.0 collective-permute-done.1
  188.1 0.0 collective-permute-done.2
  188.1 0.0 collective-permute-done.3
  188.1 2.6 collective-permute-done.4
  190.7 1.1 concatenate
  191.9 0.7 reshape.45
  192.6 9.6 %all-to-all-start.3 = ((bf16[4,5,1536]{2,1,0:T(8,128)(2,1)}), bf16[4,5,1536]{2,1,0:T(8,128)(2,1)S(1)}, u32[]{:S(2)}, u32[]{:S(2)}) async-start(bf16[4,5,1536]{2,1,0:T(8,128)(2,1)} %reshape.45), calls=%async_computation.3 | async-start | bytes 196608 | tf_op jit(solution)/shard_map/all_to_all | solution.py:70
  202.2 0.0 copy-done.7
  202.2 0.2 convolution_convert_fusion.2
  202.4 0.7 reshape.43
  203.1 12.1 %all-to-all-done.3 = bf16[4,5,1536]{2,1,0:T(8,128)(2,1)S(1)} async-done(((bf16[4,5,1536]{2,1,0:T(8,128)(2,1)}), bf16[4,5,1536]{2,1,0:T(8,128)(2,1)S(1)}, u32[]{:S(2)}, u32[]{:S(2)}) %all-to-all-start.3) | async-done | bytes 61472 | tf_op jit(solution)/shard_map/all_to_all | solution.py:70
  215.2 3.3 all-to-all-start.1
  218.5 0.3 fusion.14
  218.9 12.6 %all-to-all-done.1 = bf16[4,5,1536]{2,1,0:T(8,128)(2,1)S(1)} async-done(((bf16[4,5,1536]{2,1,0:T(8,128)(2,1)}), bf16[4,5,1536]{2,1,0:T(8,128)(2,1)S(1)}, u32[]{:S(2)}, u32[]{:S(2)}) %all-to-all-start.1) | async-done | bytes 61472 | tf_op jit(solution)/shard_map/all_to_all | solution.py:43
  231.5 0.6 broadcast_in_dim.11
  232.1 3.2 all-to-all-start.4
  235.3 5.1 %all-to-all-done.4 = f32[4,1,8]{2,1,0:T(1,128)S(1)} async-done(((f32[4,1,8]{2,1,0:T(1,128)}), f32[4,1,8]{2,1,0:T(1,128)S(1)}, u32[]{:S(2)}, u32[]{:S(2)}) %all-to-all-start.4) | async-done | bytes 160 | tf_op jit(solution)/shard_map/all_to_all | solution.py:11
  240.5 1.6 stack.3
  242.0 13.9 %all-to-all-start.2 = ((bf16[32,20,1536]{2,1,0:T(8,128)(2,1)}), bf16[32,20,1536]{2,1,0:T(8,128)(2,1)S(1)}, u32[]{:S(2)}, u32[]{:S(2)}) async-start(bf16[32,20,1536]{2,1,0:T(8,128)(2,1)} %stack.3), calls=%async_computation.2 | async-start | bytes 4718592 | tf_op jit(solution)/shard_map/all_to_all | solution.py:49
  255.9 0.0 copy-start.4
  255.9 0.5 reduce_sum.39
  256.4 0.7 broadcast_multiply_fusion
  257.1 0.7 fusion.17
  257.8 104.7 %all-to-all-done.2 = bf16[32,20,1536]{2,1,0:T(8,128)(2,1)S(1)} async-done(((bf16[32,20,1536]{2,1,0:T(8,128)(2,1)}), bf16[32,20,1536]{2,1,0:T(8,128)(2,1)S(1)}, u32[]{:S(2)}, u32[]{:S(2)}) %all-to-all-start.2) | async-done | bytes 1966112 | tf_op jit(solution)/shard_map/all_to_all | solution.py:49
  362.5 2.0 reshape.44
  364.5 0.0 copy-done.4
  364.5 0.0 copy-start.1
  364.5 0.0 copy-start.6
  364.5 3.4 fusion.1
  367.9 0.0 copy-done.1
  367.9 0.0 copy-done.6
  367.9 1.7 fusion.2
  (9 shorter events, 0.1 us)
Async XLA Ops:
  0.6 1.1 copy-start
  0.6 2.8 copy-start.2
  0.7 2.8 copy-start.5
  6.0 167.3 %copy-start.3 = (bf16[8,1536]{1,0:T(8,128)(2,1)S(1)}, bf16[8,1536]{1,0:T(8,128)(2,1)}, u32[]{:S(2)}) copy-start(bf16[8,1536]{1,0:T(8,128)(2,1)} %param.8) | copy-start | bytes 73732
  6.0 173.4 %copy-start.8 = (s32[8,2]{0,1:T(2,128)S(1)}, s32[8,2]{0,1:T(2,128)}, u32[]{:S(2)}) copy-start(s32[8,2]{0,1:T(2,128)} %param.11) | copy-start | bytes 196
  6.0 173.4 %copy-start.9 = (s32[8,2]{0,1:T(2,128)S(1)}, s32[8,2]{0,1:T(2,128)}, u32[]{:S(2)}) copy-start(s32[8,2]{0,1:T(2,128)} %param.10) | copy-start | bytes 196
  6.0 196.1 %copy-start.7 = (f32[1536]{0:T(1024)S(1)}, f32[1536]{0:T(1024)}, u32[]{:S(2)}) copy-start(f32[1536]{0:T(1024)} %param.9) | copy-start | bytes 18436
  154.9 33.2 %collective-permute-start = (bf16[24,1536]{1,0:T(8,128)(2,1)S(1)}, bf16[24,1536]{1,0:T(8,128)(2,1)S(1)}, u32[]{:S(2)}, u32[]{:S(2)}) collective-permute-start(bf16[24,1536]{1,0:T(8,128)(2,1)S(1)} %convert.10), channel_id=1, source_target_pairs={{0,1},{1,2},{2,3},{3,4},{4,5},{5,6},{6,7},{7,8},{8,9},{9,10},{10,1... | collective-permute-start | bytes 221192
  156.8 31.3 %collective-permute-start.1 = (bf16[24,1536]{1,0:T(8,128)(2,1)S(1)}, bf16[24,1536]{1,0:T(8,128)(2,1)S(1)}, u32[]{:S(2)}, u32[]{:S(2)}) collective-permute-start(bf16[24,1536]{1,0:T(8,128)(2,1)S(1)} %convert.10), channel_id=1, source_target_pairs={{0,2},{1,3},{2,4},{3,5},{4,6},{5,7},{6,8},{7,9},{8,10},{9,11},{10,... | collective-permute-start | bytes 221192
  158.1 30.0 %collective-permute-start.2 = (bf16[24,1536]{1,0:T(8,128)(2,1)S(1)}, bf16[24,1536]{1,0:T(8,128)(2,1)S(1)}, u32[]{:S(2)}, u32[]{:S(2)}) collective-permute-start(bf16[24,1536]{1,0:T(8,128)(2,1)S(1)} %convert.10), channel_id=1, source_target_pairs={{0,3},{1,4},{2,5},{3,6},{4,7},{5,8},{6,9},{7,10},{8,11},{9,12},{10... | collective-permute-start | bytes 221192
  159.4 28.7 %collective-permute-start.3 = (bf16[24,1536]{1,0:T(8,128)(2,1)S(1)}, bf16[24,1536]{1,0:T(8,128)(2,1)S(1)}, u32[]{:S(2)}, u32[]{:S(2)}) collective-permute-start(bf16[24,1536]{1,0:T(8,128)(2,1)S(1)} %convert.10), channel_id=1, source_target_pairs={{0,4},{1,5},{2,6},{3,7},{4,8},{5,9},{6,10},{7,11},{8,12},{9,13},{1... | collective-permute-start | bytes 221192
  166.9 17.8 %collective-permute-start.5 = (bf16[4,1536]{1,0:T(4,128)(2,1)S(1)}, bf16[4,1536]{1,0:T(4,128)(2,1)S(1)}, u32[]{:S(2)}, u32[]{:S(2)}) collective-permute-start(bf16[4,1536]{1,0:T(4,128)(2,1)S(1)} %slice.8), channel_id=1, source_target_pairs={{0,6},{1,7},{2,8},{3,9},{4,10},{5,11},{6,12},{7,13},{8,14},{9,15},... | collective-permute-start | bytes 36872
  174.0 10.6 %all-to-all-start = ((f32[4,1,8]{2,1,0:T(1,128)}), f32[4,1,8]{2,1,0:T(1,128)S(1)}, u32[]{:S(2)}, u32[]{:S(2)}) async-start(f32[4,1,8]{2,1,0:T(1,128)} %broadcast_in_dim.8), calls=%async_computation | async-start | bytes 4096 | tf_op jit(solution)/shard_map/all_to_all | solution.py:11
  184.7 6.1 %collective-permute-start.4 = (bf16[24,1536]{1,0:T(8,128)(2,1)S(1)}, bf16[24,1536]{1,0:T(8,128)(2,1)S(1)}, u32[]{:S(2)}, u32[]{:S(2)}) collective-permute-start(bf16[24,1536]{1,0:T(8,128)(2,1)S(1)} %convert.10), channel_id=1, source_target_pairs={{0,5},{1,6},{2,7},{3,8},{4,9},{5,10},{6,11},{7,12},{8,13},{9,14},{... | collective-permute-start | bytes 221192
  192.6 22.6 %all-to-all-start.3 = ((bf16[4,5,1536]{2,1,0:T(8,128)(2,1)}), bf16[4,5,1536]{2,1,0:T(8,128)(2,1)S(1)}, u32[]{:S(2)}, u32[]{:S(2)}) async-start(bf16[4,5,1536]{2,1,0:T(8,128)(2,1)} %reshape.45), calls=%async_computation.3 | async-start | bytes 196608 | tf_op jit(solution)/shard_map/all_to_all | solution.py:70
  215.2 16.3 %all-to-all-start.1 = ((bf16[4,5,1536]{2,1,0:T(8,128)(2,1)}), bf16[4,5,1536]{2,1,0:T(8,128)(2,1)S(1)}, u32[]{:S(2)}, u32[]{:S(2)}) async-start(bf16[4,5,1536]{2,1,0:T(8,128)(2,1)} %reshape.43), calls=%async_computation.1 | async-start | bytes 196608 | tf_op jit(solution)/shard_map/all_to_all | solution.py:43
  232.1 8.4 %all-to-all-start.4 = ((f32[4,1,8]{2,1,0:T(1,128)}), f32[4,1,8]{2,1,0:T(1,128)S(1)}, u32[]{:S(2)}, u32[]{:S(2)}) async-start(f32[4,1,8]{2,1,0:T(1,128)} %broadcast_in_dim.11), calls=%async_computation.4 | async-start | bytes 4096 | tf_op jit(solution)/shard_map/all_to_all | solution.py:11
  242.0 120.4 %all-to-all-start.2 = ((bf16[32,20,1536]{2,1,0:T(8,128)(2,1)}), bf16[32,20,1536]{2,1,0:T(8,128)(2,1)S(1)}, u32[]{:S(2)}, u32[]{:S(2)}) async-start(bf16[32,20,1536]{2,1,0:T(8,128)(2,1)} %stack.3), calls=%async_computation.2 | async-start | bytes 4718592 | tf_op jit(solution)/shard_map/all_to_all | solution.py:49
  255.9 108.6 %copy-start.4 = (bf16[1,640,256]{2,1,0:T(8,128)(2,1)S(1)}, bf16[1,640,256]{2,1,0:T(8,128)(2,1)}, u32[]{:S(2)}) copy-start(bf16[1,640,256]{2,1,0:T(8,128)(2,1)} %param.14) | copy-start | bytes 983044
  364.5 3.4 copy-start.1
  364.5 3.4 copy-start.6
